TPU v7x, 128 devices: a whole 4x4x4 slice. The times are simulated.
128 devices in a mesh: dev: 128 (over z, y, x, core).
Axes of the slice: x: 4, y: 4, z: 4, core: 2. Of those that a mesh axis runs over, the one named last changes fastest.
Arguments:
- samples: bfloat16 [1024, 201216], P('dev'), may hold values from -6 to 6
- input_gain: float32 [1024], P('dev'), may hold values from 0.3 to 4, as said below
Outputs:
- visibility: bfloat16 [768, 36, 2, 128, 128], P('dev')
Inputs may be any that keep to these rules, and one draw needn't show every extreme that they name: `input_gain`: positive gains, one for each input.
All inputs are finite; a program needn't handle non-finite values.
Results may differ from a plain program's by a relative error of at most 0.0071.
Values may be sent and summed in bfloat16 or wider, within the bound.
No kernel may reach another device: no remote copies, remote signals or barrier semaphores. Data moves between devices by JAX's collectives and lax.ppermute only.
A program may use at most 128 MiB of HBM per device.

v0:
```python
import math

import jax
import jax.numpy as jnp
import numpy as np
from jax import lax
from jax.sharding import PartitionSpec as P

INPUTS = 1024
FRAME = 1536
TAPS = 4
BLOCK = 128


def pfb_window(frame_len, taps):
    total = taps * frame_len
    position = jnp.arange(total, dtype=jnp.int32).astype(jnp.float32)
    centred = (position - total / 2 + 0.5) / frame_len
    taper = 0.54 - 0.46 * jnp.cos(2.0 * math.pi * position / (total - 1))
    return (jnp.sinc(centred) * taper).reshape(taps, frame_len)


def dft_table(frame_len):
    channels = frame_len // 2
    sample_idx = jnp.arange(frame_len, dtype=jnp.int32)
    chan_idx = jnp.arange(channels, dtype=jnp.int32)
    phase = sample_idx[:, None] * chan_idx[None, :] % frame_len
    angle = 2.0 * math.pi / frame_len * phase.astype(jnp.float32)
    norm_factor = 1.0 / math.sqrt(frame_len)
    table = jnp.concatenate([jnp.cos(angle), -jnp.sin(angle)], axis=1) * norm_factor
    return table.astype(jnp.bfloat16)


def correlate(received):
    chans = received[0]
    count = chans.shape[0]
    inputs = chans.shape[1]
    width = chans.shape[2]
    spectra = width // 2
    nblk = inputs // BLOCK
    rows_np, cols_np = np.triu_indices(nblk)
    rows_idx = jnp.asarray(rows_np.astype(np.int32))
    cols_idx = jnp.asarray(cols_np.astype(np.int32))
    tiles = chans.reshape(count, nblk, BLOCK, width)
    left = jnp.take(tiles, rows_idx, axis=1)
    right = jnp.take(tiles, cols_idx, axis=1)
    turned = jnp.concatenate([-right[..., spectra:], right[..., :spectra]], axis=-1)
    real_part = jnp.einsum("kpis,kpjs->kpij", left, right, preferred_element_type=jnp.float32)
    imag_part = jnp.einsum("kpis,kpjs->kpij", left, turned, preferred_element_type=jnp.float32)
    stacked = jnp.stack([real_part, imag_part], axis=2) * (1.0 / spectra)
    return stacked.astype(jnp.bfloat16)


def local(samples, input_gain):
    num_dev = lax.axis_size("dev")
    local_inputs = samples.shape[0]
    frame_len = FRAME
    taps = TAPS
    channels = frame_len // 2
    spectra = samples.shape[1] // frame_len - taps + 1
    local_chans = channels // num_dev
    window = pfb_window(frame_len, taps)
    table = dft_table(frame_len)
    frames = samples.reshape(local_inputs, spectra + taps - 1, frame_len)
    acc = jnp.zeros((local_inputs, spectra, frame_len), jnp.float32)
    for tap in range(taps):
        acc = acc + window[tap][None, None, :] * frames[:, tap : tap + spectra, :].astype(
            jnp.float32
        )
    filtered = acc.astype(jnp.bfloat16).reshape(local_inputs * spectra, frame_len)
    spectrum = jnp.dot(filtered, table, preferred_element_type=jnp.float32)
    spectrum = (
        spectrum.reshape(local_inputs, spectra, 2, channels) * input_gain[:, None, None, None]
    )
    partial_power = jnp.sum(spectrum * spectrum, axis=(0, 1, 2))
    power = lax.psum(partial_power, "dev")
    level = 1.0 / jnp.sqrt(power / (INPUTS * spectra) + 1e-06)
    quantized = (spectrum * level[None, None, None, :]).astype(jnp.bfloat16)
    outgoing = quantized.reshape(local_inputs, spectra, 2, num_dev, local_chans)
    outgoing = outgoing.transpose(3, 4, 0, 2, 1).reshape(
        num_dev, local_chans, local_inputs, 2 * spectra
    )
    visibility = correlate(lax.all_to_all(outgoing, "dev", split_axis=0, concat_axis=2, tiled=True))
    return visibility


def solution(mesh):
    in_specs = (P("dev", None), P("dev"))
    out_specs = P("dev", None, None, None, None)
    return jax.shard_map(local, mesh=mesh, in_specs=in_specs, out_specs=out_specs, check_vma=False)
```

profile of v0, /device:TPU:1, one launch (start us, length us, event | category | flops | bytes accessed | tf_op | source)
XLA Modules:
  0.0 248.8 jit_solution(2394168002015564757)
XLA Ops:
  0.0 19.1 %sine_negate_fusion = (f32[1536,768]{0,1:T(8,128)S(1)}, f32[1536,768]{0,1:T(8,128)S(1)}) fusion(), kind=kLoop, calls=%fused_computation.23 | loop fusion | flops 11796480 | bytes 9437184 | tf_op jit(solution)/shard_map/neg | solution.py:30
  19.1 0.1 fusion.38
  19.3 4.7 %fusion.48 = (bf16[8,128,1536]{2,0,1:T(8,128)(2,1)}, bf16[8,128,1536]{2,0,1:T(8,128)(2,1)}, bf16[8,128,1536]{2,0,1:T(8,128)(2,1)}, bf16[8,128,1536]{2,0,1:T(8,128)(2,1)}) fusion(bf16[8,131,1536]{2,0,1:T(8,128)(2,1)S(1)} %bitcast.41), kind=kLoop, calls=%fused_computation.67 | loop fusion | bytes 25165824 | tf_op jit(solution)/shard_map/slice | solution.py:67
  23.9 0.0 copy-start.3
  24.0 3.5 %fusion.8 = bf16[1536,1536]{0,1:T(8,128)(2,1)} fusion(f32[1536,768]{0,1:T(8,128)S(1)} %get-tuple-element.18, f32[1536,768]{0,1:T(8,128)S(1)} %get-tuple-element.19), kind=kLoop, calls=%fused_computation.13 | loop fusion | flops 7077888 | bytes 14155776 | tf_op jit(solution)/shard_map/convert_element_type | solution.py:31
  27.5 23.0 %multiply_reduce_fusion = (f32[768]{0:T(1024)S(1)}, f32[8,128,2,768]{3,1,2,0:T(8,128)}) fusion(f32[8]{0:T(128)S(1)} %copy-done.3, bf16[2,768,1536,1]{2,1,0,3:T(8,128)(2,1)} %bitcast.44, bf16[8,128,1536]{2,0,1:T(8,128)(2,1)} %get-tuple-element.11, bf16[8,128,1536]{2,0,1:T(8,128)(2,1)} %get-tuple-element.9, bf16[8,128,1536]{2,0,1:T(8,128)(2,1)} %get-tuple-element.10, ...), kind=kOutput, calls=%fused_computation.19 | convolution fusion | flops 4855430144 | bytes 23620640 | tf_op jit(solution)/shard_map/dot_general | solution.py:71
  50.5 68.6 %psum.7 = f32[768]{0:T(1024)S(1)} all-reduce(f32[768]{0:T(1024)S(1)} %get-tuple-element.16), channel_id=1, replica_groups=mesh['dev'=128] {'dev'}, use_global_device_ids=true, to_apply=%region_1.2 | all-reduce | flops 768 | bytes 6144 | tf_op jit(solution)/shard_map/psum | solution.py:76
  119.1 3.6 %multiply_convert_fusion = bf16[8,128,2,768]{3,1,2,0:T(8,128)(2,1)S(1)} fusion(f32[8,128,2,768]{3,1,2,0:T(8,128)} %get-tuple-element.17, f32[768]{0:T(1024)S(1)} %add_rsqrt_fusion, f32[8]{0:T(128)S(1)} %copy-done.3), kind=kLoop, calls=%fused_computation.18 | loop fusion | flops 4718592 | bytes 9440288 | tf_op jit(solution)/shard_map/convert_element_type | solution.py:78
  122.7 0.0 copy-start.4
  122.7 0.0 copy-start.5
  122.7 3.4 %copy.31 = bf16[8,128,2,768]{1,0,2,3:T(8,128)(2,1)} copy(bf16[8,128,2,768]{3,1,2,0:T(8,128)(2,1)S(1)} %multiply_convert_fusion) | data formatting | bytes 6291456 | tf_op jit(solution)/shard_map/transpose | solution.py:80
  126.1 4.7 %all-to-all-start = ((bf16[128,6,8,256]{3,2,1,0:T(8,128)(2,1)}), bf16[128,6,8,256]{3,2,1,0:T(8,128)(2,1)S(1)}, u32[]{:S(2)}, u32[]{:S(2)}) async-start(bf16[128,6,8,256]{3,2,1,0:T(8,128)(2,1)} %bitcast.43), calls=%async_computation | async-start | bytes 6291456 | tf_op jit(solution)/shard_map/all_to_all | solution.py:83
  130.8 41.4 %all-to-all-done = bf16[128,6,8,256]{3,2,1,0:T(8,128)(2,1)S(1)} async-done(((bf16[128,6,8,256]{3,2,1,0:T(8,128)(2,1)}), bf16[128,6,8,256]{3,2,1,0:T(8,128)(2,1)S(1)}, u32[]{:S(2)}, u32[]{:S(2)}) %all-to-all-start) | async-done | bytes 3145760 | tf_op jit(solution)/shard_map/all_to_all | solution.py:83
  172.2 1.7 copy-done.2
  173.9 2.1 copy.25
  176.0 7.3 %gather_fusion.1 = bf16[36,6,128,256]{3,2,1,0:T(8,128)(2,1)} fusion(bf16[6,8,128,256]{3,2,1,0:T(8,128)(2,1)S(1)} %bitcast.38, s32[1024]{0:T(1024)S(1)} %pad_clamp_fusion), kind=kCustom, calls=%fused_computation.1.clone | custom fusion | bytes 28311696 | tf_op jit(solution)/shard_map/jit(_take)/gather | solution.py:46
  183.3 6.9 %copy.70 = bf16[36,6,128,256]{3,2,0,1:T(8,128)(2,1)S(1)} copy(bf16[36,6,128,256]{3,2,1,0:T(8,128)(2,1)} %gather_fusion.1) | data formatting | bytes 28311552 | tf_op jit(solution)/shard_map/jit(_take)/gather | solution.py:46
  190.2 5.5 %slice_negate_fusion = (bf16[6,36,128,128]{3,2,1,0:T(8,128)(2,1)}, bf16[6,36,128,128]{3,2,1,0:T(8,128)(2,1)}) fusion(bf16[6,36,128,256]{3,2,1,0:T(8,128)(2,1)S(1)} %bitcast.40), kind=kLoop, calls=%fused_computation.16 | loop fusion | flops 3538944 | bytes 28311552 | tf_op jit(solution)/shard_map/neg | solution.py:47
  195.7 7.3 %gather_fusion = bf16[36,6,128,256]{3,2,1,0:T(8,128)(2,1)} fusion(bf16[6,8,128,256]{3,2,1,0:T(8,128)(2,1)S(1)} %bitcast.39, s32[1024]{0:T(1024)S(1)} %pad_clamp_fusion.1), kind=kCustom, calls=%fused_computation.clone | custom fusion | bytes 28311696 | tf_op jit(solution)/shard_map/jit(_take)/gather | solution.py:45
  203.0 16.6 %fusion.14 = f32[6,36,1,128,128]{4,3,1,0,2:T(8,128)} fusion(bf16[36,6,128,256]{3,2,1,0:T(8,128)(2,1)} %gather_fusion.1, bf16[36,6,128,256]{3,2,1,0:T(8,128)(2,1)} %gather_fusion), kind=kOutput, calls=%fused_computation.15 | convolution fusion | flops 1811939328 | bytes 42467328 | tf_op jit(solution)/shard_map/kpis,kpjs->kpij/dot_general | solution.py:48
  219.6 1.7 copy-done
  221.3 10.4 %fusion.9 = f32[6,36,1,128,128]{4,3,1,0,2:T(8,128)} fusion(bf16[6,36,128,128]{3,2,1,0:T(8,128)(2,1)} %get-tuple-element.7, bf16[6,36,128,128]{3,2,1,0:T(8,128)(2,1)} %get-tuple-element.6, bf16[36,6,128,256]{3,2,1,0:T(8,128)(2,1)S(1)} %copy-done), kind=kOutput, calls=%fused_computation.14 | convolution fusion | flops 1840250880 | bytes 42467328 | tf_op jit(solution)/shard_map/kpis,kpjs->kpij/dot_general | solution.py:49
  231.7 11.6 %fusion = bf16[6,36,2,128,128]{4,3,1,0,2:T(8,128)(2,1)S(1)} fusion(f32[6,36,1,128,128]{4,3,1,0,2:T(8,128)} %fusion.9, f32[6,36,1,128,128]{4,3,1,0,2:T(8,128)} %fusion.14), kind=kLoop, calls=%fused_computation.3 | loop fusion | flops 21233664 | bytes 42467328 | tf_op jit(solution)/shard_map/convert_element_type | solution.py:51
  243.3 5.5 %copy.29 = bf16[6,36,2,128,128]{4,3,2,1,0:T(8,128)(2,1)} copy(bf16[6,36,2,128,128]{4,3,1,0,2:T(8,128)(2,1)S(1)} %fusion) | data formatting | bytes 28311552 | tf_op jit(solution)/shard_map/convert_element_type | solution.py:51
  (11 shorter events, 0.0 us)
Async XLA Ops:
  0.0 19.3 %copy-start.1 = (bf16[8,201216]{1,0:T(8,128)(2,1)S(1)}, bf16[8,201216]{1,0:T(8,128)(2,1)}, u32[]{:S(2)}) copy-start(bf16[8,201216]{1,0:T(8,128)(2,1)} %param.6) | copy-start | bytes 9658372
  23.9 3.5 %copy-start.3 = (f32[8]{0:T(128)S(1)}, f32[8]{0:T(128)}, u32[]{:S(2)}) copy-start(f32[8]{0:T(128)} %param.7) | copy-start | bytes 100
  122.7 8.1 %copy-start.4 = (s32[36]{0:T(128)S(1)}, s32[36]{0:T(128)}, u32[]{:S(2)}) copy-start(s32[36]{0:T(128)} %constant.118) | copy-start | bytes 436
  122.7 8.1 %copy-start.5 = (s32[36]{0:T(128)S(1)}, s32[36]{0:T(128)}, u32[]{:S(2)}) copy-start(s32[36]{0:T(128)} %constant.117) | copy-start | bytes 436
  126.1 46.2 %all-to-all-start = ((bf16[128,6,8,256]{3,2,1,0:T(8,128)(2,1)}), bf16[128,6,8,256]{3,2,1,0:T(8,128)(2,1)S(1)}, u32[]{:S(2)}, u32[]{:S(2)}) async-start(bf16[128,6,8,256]{3,2,1,0:T(8,128)(2,1)} %bitcast.43), calls=%async_computation | async-start | bytes 6291456 | tf_op jit(solution)/shard_map/all_to_all | solution.py:83
  172.2 1.7 copy-start.2
  203.0 18.3 %copy-start = (bf16[36,6,128,256]{3,2,1,0:T(8,128)(2,1)S(1)}, bf16[36,6,128,256]{3,2,1,0:T(8,128)(2,1)}, u32[]{:S(2)}) copy-start(bf16[36,6,128,256]{3,2,1,0:T(8,128)(2,1)} %gather_fusion) | copy-start | bytes 42467332
where the time goes:
time: 249 us
  blocking collectives  68.6 us (28%)
  matrix products  49.9 us (20%)
  other arithmetic  43.5 us (17%)
  waiting for transfers between devices  41.4 us (17%)
  local copies, waits for them, and re-layouts  40.5 us (16%)
  starting transfers between devices  4.69 us (2%)
    psum x1, blocking collectives, local(): power = lax.psum(partial_power, 'dev')  68.6 us
    all_to_all x1, waiting for transfers between devices, local(): lax.all_to_all(outgoing, 'dev', split_axis=0, concat_axis=2, tiled=True)  41.4 us
    dot_general x1, matrix products, local(): spectrum = jnp.dot(filtered, table, preferred_element_type=jnp.float32)  23 us
    neg x1, other arithmetic, dft_table(): -jnp.sin(angle)  19.1 us
    dot_general x1, matrix products, correlate(): jnp.einsum('kpis,kpjs->kpij', left, right, preferred_element_type=jnp.flo...  16.6 us
    gather x2, local copies, waits for them, and re-layouts, correlate(): right = jnp.take(tiles, cols_idx, axis=1)  14.2 us
    convert_element_type x1, other arithmetic, correlate(): return stacked.astype(jnp.bfloat16)  11.6 us
    dot_general x1, matrix products, correlate(): jnp.einsum('kpis,kpjs->kpij', left, turned, preferred_element_type=jnp.fl...  10.4 us
  transfers between devices with their start and end apart: 1, of which 1 were waited for; matrix products, arithmetic and copies ran while one was open for 0% of the time, Pallas kernels for 0%

commit v1 on v0

v1 whole, which is shorter than its diff:
```python
import functools
import math

import jax
import jax.numpy as jnp
import numpy as np
from jax import lax
from jax.experimental import pallas as pl
from jax.experimental.pallas import tpu as pltpu
from jax.sharding import PartitionSpec as P

INPUTS = 1024
FRAME = 1536
TAPS = 4
SPECTRA = 128
BLOCK = 128
CHANNELS = 768
DEVICES = 128
LOCAL = INPUTS // DEVICES
OWNED = CHANNELS // DEVICES
HALF = FRAME // 2
NBLK = INPUTS // BLOCK
SCALE = 1024.0
F32 = jnp.float32
BF16 = jnp.bfloat16
NT = (((1,), (1,)), ((), ()))


def pfb_window():
    total = TAPS * FRAME
    position = np.arange(total, dtype=np.float64)
    centred = (position - total / 2 + 0.5) / FRAME
    taper = 0.54 - 0.46 * np.cos(2.0 * math.pi * position / (total - 1))
    return (np.sinc(centred) * taper).reshape(TAPS, FRAME).astype(np.float32)


def twiddles():
    owner = np.outer(np.arange(DEVICES), np.arange(256)) % 256 * (2.0 * math.pi / 256)
    own = np.outer(np.arange(OWNED), np.arange(HALF)) % FRAME * (2.0 * math.pi / FRAME)
    norm = 1.0 / math.sqrt(FRAME)
    coarse = np.stack([np.cos(owner), -np.sin(owner)]) * norm
    fine = np.stack([np.cos(own), -np.sin(own)])
    return coarse.astype(np.float32), fine.astype(np.float32)


def make_table(parity, coarse_ref, fine_ref, table_ref):
    for block in range(HALF // 256):
        lanes = slice(block * 256, block * 256 + 256)
        re = coarse_ref[0]
        im = coarse_ref[1]
        for m in range(OWNED // 2):
            j = 2 * m + parity
            fre = fine_ref[0, j : j + 1, lanes]
            fim = fine_ref[1, j : j + 1, lanes]
            base = m * 2 * DEVICES
            table_ref[base : base + DEVICES, lanes] = (re * fre - im * fim).astype(BF16)
            table_ref[base + DEVICES : base + 2 * DEVICES, lanes] = (re * fim + im * fre).astype(BF16)


def transform(table_ref, folded_ref, gain_ref, out_ref, turned_ref):
    for pair in range(LOCAL // 2):
        rows = folded_ref[pair * 256 : pair * 256 + 256, :]
        for m in range(OWNED // 2):
            base = m * 2 * DEVICES
            spec = lax.dot_general(table_ref[base : base + 2 * DEVICES, :], rows, NT, preferred_element_type=F32)
            for side in range(2):
                i = 2 * pair + side
                gain = gain_ref[i] * SCALE
                for ri in range(2):
                    turned_ref[ri, pl.ds(m * LOCAL + i, DEVICES, stride=3 * LOCAL)] = (
                        spec[ri * DEVICES : (ri + 1) * DEVICES, side * SPECTRA : (side + 1) * SPECTRA] * gain
                    )
    for ri in range(2):
        out_ref[..., ri * SPECTRA : (ri + 1) * SPECTRA] = turned_ref[ri].reshape(DEVICES, OWNED // 2, LOCAL, SPECTRA).astype(BF16)


def filter_kernel(frames_ref, window_ref, coarse_ref, fine_ref, gain_ref, out_ref, odd_ref, even_ref, sum_ref, dif_ref, table_ref, turned_ref):
    step = 16
    width = 128

    def body(b, carry):
        s0 = b * step
        for block in range(HALF // width):
            acc = []
            for half in range(2):
                lanes = slice(half * HALF + block * width, half * HALF + block * width + width)
                frames = frames_ref[pl.ds(s0, step + TAPS - 1), :, lanes].astype(F32)
                total = window_ref[0, lanes][None, None, :] * frames[0:step]
                for tap in range(1, TAPS):
                    total = total + window_ref[tap, lanes][None, None, :] * frames[tap : tap + step]
                acc.append(total.reshape(step * LOCAL, width))
            here = pl.ds(pl.multiple_of(s0 * LOCAL, step * LOCAL), step * LOCAL)
            sum_ref[block, here] = acc[0] + acc[1]
            dif_ref[block, here] = acc[0] - acc[1]
        return carry

    lax.fori_loop(0, SPECTRA // step, body, 0)
    make_table(0, coarse_ref, fine_ref, table_ref)
    for i in range(LOCAL):
        for block in range(HALF // width):
            lanes = slice(block * width, block * width + width)
            mine = slice(i * SPECTRA, (i + 1) * SPECTRA)
            even_ref[mine, lanes] = sum_ref[block, pl.ds(i, SPECTRA, stride=LOCAL)].astype(BF16)
            odd_ref[mine, lanes] = dif_ref[block, pl.ds(i, SPECTRA, stride=LOCAL)].astype(BF16)
    transform(table_ref, even_ref, gain_ref, out_ref, turned_ref)


def odd_kernel(odd_ref, coarse_ref, fine_ref, gain_ref, out_ref, table_ref, turned_ref):
    make_table(1, coarse_ref, fine_ref, table_ref)
    transform(table_ref, odd_ref, gain_ref, out_ref, turned_ref)


def gram_kernel(spectra_ref, *refs):
    out_ref = refs[-1]
    volt = spectra_ref[...].reshape(INPUTS, 2 * SPECTRA)
    wide = volt.astype(F32)
    power = jnp.sum(wide * wide, keepdims=True) * (1.0 / (SCALE * SCALE))
    scale = (1.0 / (power / (INPUTS * SPECTRA) + 1e-06)) * (1.0 / (SCALE * SCALE * SPECTRA))
    for cols in range(NBLK // 2):
        right = volt[cols * 256 : cols * 256 + 256]
        turned = jnp.concatenate([-right[:, SPECTRA:], right[:, :SPECTRA]], axis=1)
        both = jnp.concatenate([right, turned], axis=0)
        height = (2 * cols + 2) * BLOCK
        tiles = lax.dot_general(volt[:height], both, NT, preferred_element_type=F32)
        tiles = (tiles * scale).astype(BF16)
        for r in range(2 * cols + 2):
            for side in range(2):
                c = 2 * cols + side
                if c < r:
                    continue
                p = r * NBLK - r * (r - 1) // 2 + c - r
                for ri in range(2):
                    at = ri * 256 + side * BLOCK
                    out_ref[p, ri] = tiles[r * BLOCK : (r + 1) * BLOCK, at : at + BLOCK]


def vmem(*shape):
    return pl.BlockSpec(memory_space=pltpu.VMEM)


def gram(parity, received, out=None):
    npair = NBLK * (NBLK + 1) // 2
    shape = jax.ShapeDtypeStruct((OWNED, npair, 2, BLOCK, BLOCK), BF16)
    args = [received]
    in_specs = [pl.BlockSpec((DEVICES, None, LOCAL, 2 * SPECTRA), lambda m: (0, m, 0, 0))]
    if out is not None:
        args.append(out)
        in_specs.append(pl.BlockSpec(memory_space=pl.ANY))
    return pl.pallas_call(
        gram_kernel,
        name=f"gram{parity}",
        grid=(OWNED // 2,),
        in_specs=in_specs,
        out_specs=pl.BlockSpec((None, npair, 2, BLOCK, BLOCK), lambda m: (2 * m + parity, 0, 0, 0, 0)),
        out_shape=shape,
        input_output_aliases={} if out is None else {1: 0},
        compiler_params=pltpu.CompilerParams(vmem_limit_bytes=48 << 20),
    )(*args)


def local(samples, input_gain):
    frames = samples.reshape(LOCAL, SPECTRA + TAPS - 1, FRAME).transpose(1, 0, 2)
    coarse, fine = (jnp.asarray(t) for t in twiddles())
    window = jnp.asarray(pfb_window())
    sent = jax.ShapeDtypeStruct((DEVICES, OWNED // 2, LOCAL, 2 * SPECTRA), BF16)
    rows = LOCAL * SPECTRA
    table = pltpu.VMEM((OWNED * DEVICES, HALF), BF16)
    turned = pltpu.VMEM((2, DEVICES * OWNED // 2 * LOCAL, SPECTRA), F32)
    folds = pltpu.VMEM((HALF // 128, rows, 128), F32)
    smem = pl.BlockSpec(memory_space=pltpu.SMEM)
    params = pltpu.CompilerParams(vmem_limit_bytes=48 << 20)
    even, folded = pl.pallas_call(
        filter_kernel,
        name="filter",
        in_specs=[vmem()] * 4 + [smem],
        out_specs=[vmem()] * 2,
        out_shape=[sent, jax.ShapeDtypeStruct((rows, HALF), BF16)],
        scratch_shapes=[pltpu.VMEM((rows, HALF), BF16), folds, folds, table, turned],
        compiler_params=params,
    )(frames, window, coarse, fine, input_gain)
    move = functools.partial(lax.all_to_all, axis_name="dev", split_axis=0, concat_axis=0, tiled=True)
    even = move(even)
    odd = pl.pallas_call(
        odd_kernel,
        name="odd",
        in_specs=[vmem()] * 3 + [smem],
        out_specs=vmem(),
        out_shape=sent,
        scratch_shapes=[table, turned],
        compiler_params=params,
    )(folded, coarse, fine, input_gain)
    odd = move(odd)
    return gram(1, odd, gram(0, even))


def solution(mesh):
    in_specs = (P("dev", None), P("dev"))
    out_specs = P("dev", None, None, None, None)
    return jax.shard_map(local, mesh=mesh, in_specs=in_specs, out_specs=out_specs, check_vma=False)
```

time: 249 us -> 82.3 us (0.33)
  blocking collectives: 68.6 us -> 0 us
  matrix products: 49.9 us -> 0 us
  other arithmetic: 43.5 us -> 0 us
  local copies, waits for them, and re-layouts: 40.5 us -> 4.29 us
  Pallas kernels: 0 us -> 20.6 us
  starting transfers between devices: 4.69 us -> 15.9 us
    psum x1 -> x0, blocking collectives: 68.6 us -> none  [local(): power = lax.psum(partial_power, 'dev')]
    dot_general x3 -> x0, matrix products: 49.9 us -> none  [the longest x1 23 us: local(): spectrum = jnp.dot(filtered, table, preferred_element_type=jnp.float32)]
    neg x2 -> x0, other arithmetic: 24.6 us -> none  [the longest x1 19.1 us: dft_table(): -jnp.sin(angle)]
    gather x3 -> x0, local copies, waits for them, and re-layouts: 21.5 us -> none  [the longest x2 14.2 us: correlate(): right = jnp.take(tiles, cols_idx, axis=1)]
    pallas_call x0 -> x4, Pallas kernels: none -> 20.6 us  [the longest x2 10.4 us: gram(): pl.pallas_call(gram_kernel, name=f'gram{parity}', grid=(OWNED // 2,), in_...]
    convert_element_type x3 -> x0, other arithmetic: 18.7 us -> none  [the longest x1 11.6 us: correlate(): return stacked.astype(jnp.bfloat16)]
    all_to_all x1 -> x2, starting transfers between devices: 4.69 us -> 15.9 us  [the longest x1 11.5 us: local(): even = move(even)]
    convert_element_type x1 -> x0, local copies, waits for them, and re-layouts: 5.48 us -> none  [correlate(): return stacked.astype(jnp.bfloat16)]
  transfers between devices with their start and end apart: 1 -> 2, of which waited for: 1 -> 2; matrix products, arithmetic and copies ran while one was open for 0% -> 0% of each run, Pallas kernels for 0% -> 11%
where the time goes in v1:
time: 82.3 us; the launch traced here: 81.9 us
  waiting for transfers between devices  41.1 us (50%)
  Pallas kernels  20.6 us (25%)
  starting transfers between devices  15.9 us (19%)
  local copies, waits for them, and re-layouts  4.29 us (5%)
    all_to_all x1, waiting for transfers between devices, local(): even = move(even)  21.3 us
    all_to_all x1, waiting for transfers between devices, local(): odd = move(odd)  19.8 us
    all_to_all x1, starting transfers between devices, local(): even = move(even)  11.5 us
    pallas_call x2, Pallas kernels, gram(): pl.pallas_call(gram_kernel, name=f'gram{parity}', grid=(OWNED // 2,), in_...  10.4 us
    pallas_call x1, Pallas kernels, local(): pl.pallas_call(filter_kernel, name='filter', in_specs=[vmem()] * 4 + [sme...  6.7 us
    all_to_all x1, starting transfers between devices, local(): odd = move(odd)  4.4 us
    unnamed x16, local copies, waits for them, and re-layouts  4.29 us
    pallas_call x1, Pallas kernels, local(): pl.pallas_call(odd_kernel, name='odd', in_specs=[vmem()] * 3 + [smem], ou...  3.53 us
  transfers between devices with their start and end apart: 2, of which 2 were waited for; matrix products, arithmetic and copies ran while one was open for 0% of the time, Pallas kernels for 11%

profile of v1, /device:TPU:1, one launch (start us, length us, event | category | flops | bytes accessed | tf_op | source)
XLA Modules:
  0.0 81.9 jit_solution(2093982864752605568)
XLA Ops:
  0.0 0.0 copy-start.1
  0.0 0.9 %copy-done.1 = f32[2,128,256]{2,1,0:T(8,128)S(1)} copy-done((f32[2,128,256]{2,1,0:T(8,128)S(1)}, f32[2,128,256]{2,1,0:T(8,128)}, u32[]{:S(2)}) %copy-start.1) | copy-done | bytes 262168
  1.0 0.0 copy-start.3
  1.0 0.8 copy-done.3
  1.8 0.0 copy-start.5
  1.8 0.7 copy-done.5
  2.5 0.0 copy-start.6
  2.5 0.7 copy-done.6
  3.1 6.7 %filter.1 = (bf16[128,3,8,256]{3,2,1,0:T(8,128)(2,1)S(1)}, bf16[1024,768]{1,0:T(8,128)(2,1)S(1)}) custom-call(bf16[131,8,1536]{2,1,0:T(8,128)(2,1)} %bitcast.3, f32[4,1536]{1,0:T(4,128)S(1)} %copy-done.5, f32[2,128,256]{2,1,0:T(8,128)S(1)} %copy-done.1, f32[2,6,768]{2,1,0:T(8,128)S(1)} %copy-done.3, f32[8]{0:T(128)S(1)} %copy-done.6), custom_call_target="tpu_custom_call" | custom-call | tf_op jit(solution)/shard_map/filter/pallas_call | solution.py:172
  9.8 0.0 copy-start
  9.9 1.1 %copy-done = bf16[128,3,8,256]{3,2,1,0:T(8,128)(2,1)} copy-done((bf16[128,3,8,256]{3,2,1,0:T(8,128)(2,1)}, bf16[128,3,8,256]{3,2,1,0:T(8,128)(2,1)S(1)}, u32[]{:S(2)}) %copy-start) | copy-done | bytes 1572888
  11.0 0.0 copy-start.2
  11.0 0.0 copy-start.4
  11.0 0.0 copy-start.7
  11.0 11.5 %all-to-all-start.1 = ((bf16[128,3,8,256]{3,2,1,0:T(8,128)(2,1)}), bf16[128,3,8,256]{3,2,1,0:T(8,128)(2,1)S(1)}, u32[]{:S(2)}, u32[]{:S(2)}) async-start(bf16[128,3,8,256]{3,2,1,0:T(8,128)(2,1)} %copy-done), calls=%async_computation.1 | async-start | bytes 3145728 | tf_op jit(solution)/shard_map/all_to_all | solution.py:182
  22.5 0.0 copy-done.2
  22.5 0.0 copy-done.4
  22.5 0.0 copy-done.7
  22.5 3.5 %odd.1 = bf16[128,3,8,256]{3,2,1,0:T(8,128)(2,1)} custom-call(bf16[1024,768]{1,0:T(8,128)(2,1)S(1)} %get-tuple-element.7.odd_ref, f32[2,128,256]{2,1,0:T(8,128)S(1)} %copy-done.2, f32[2,6,768]{2,1,0:T(8,128)S(1)} %copy-done.4, f32[8]{0:T(128)S(1)} %copy-done.7), custom_call_target="tpu_custom_call" | custom-call | tf_op jit(solution)/shard_map/odd/pallas_call | solution.py:183
  26.1 21.3 %all-to-all-done.1.spectra_ref = bf16[128,3,8,256]{3,2,1,0:T(8,128)(2,1)S(1)} async-done(((bf16[128,3,8,256]{3,2,1,0:T(8,128)(2,1)}), bf16[128,3,8,256]{3,2,1,0:T(8,128)(2,1)S(1)}, u32[]{:S(2)}, u32[]{:S(2)}) %all-to-all-start.1) | async-done | bytes 1572896 | tf_op jit(solution)/shard_map/all_to_all | solution.py:182
  47.3 4.4 %all-to-all-start = ((bf16[128,3,8,256]{3,2,1,0:T(8,128)(2,1)}), bf16[128,3,8,256]{3,2,1,0:T(8,128)(2,1)S(1)}, u32[]{:S(2)}, u32[]{:S(2)}) async-start(bf16[128,3,8,256]{3,2,1,0:T(8,128)(2,1)} %odd.1), calls=%async_computation | async-start | bytes 3145728 | tf_op jit(solution)/shard_map/all_to_all | solution.py:192
  51.7 5.2 %gram0.1.refs_0_ = bf16[6,36,2,128,128]{4,3,2,1,0:T(8,128)(2,1)} custom-call(bf16[128,3,8,256]{3,2,1,0:T(8,128)(2,1)S(1)} %all-to-all-done.1.spectra_ref), custom_call_target="tpu_custom_call" | custom-call | tf_op jit(solution)/shard_map/gram0/pallas_call | solution.py:149
  56.9 19.8 %all-to-all-done.spectra_ref = bf16[128,3,8,256]{3,2,1,0:T(8,128)(2,1)S(1)} async-done(((bf16[128,3,8,256]{3,2,1,0:T(8,128)(2,1)}), bf16[128,3,8,256]{3,2,1,0:T(8,128)(2,1)S(1)}, u32[]{:S(2)}, u32[]{:S(2)}) %all-to-all-start) | async-done | bytes 1572896 | tf_op jit(solution)/shard_map/all_to_all | solution.py:192
  76.7 5.2 %gram1.1 = bf16[6,36,2,128,128]{4,3,2,1,0:T(8,128)(2,1)} custom-call(bf16[128,3,8,256]{3,2,1,0:T(8,128)(2,1)S(1)} %all-to-all-done.spectra_ref, bf16[6,36,2,128,128]{4,3,2,1,0:T(8,128)(2,1)} %gram0.1.refs_0_), custom_call_target="tpu_custom_call", output_to_operand_aliasing={{}: (1, {})} | custom-call | tf_op jit(solution)/shard_map/gram1/pallas_call | solution.py:149
Async XLA Ops:
  0.0 0.9 %copy-start.1 = (f32[2,128,256]{2,1,0:T(8,128)S(1)}, f32[2,128,256]{2,1,0:T(8,128)}, u32[]{:S(2)}) copy-start(f32[2,128,256]{2,1,0:T(8,128)} %constant.6.clone.coarse_ref) | copy-start | bytes 786436
  1.0 0.8 copy-start.3
  1.8 0.7 copy-start.5
  2.5 0.7 copy-start.6
  9.8 1.1 %copy-start = (bf16[128,3,8,256]{3,2,1,0:T(8,128)(2,1)}, bf16[128,3,8,256]{3,2,1,0:T(8,128)(2,1)S(1)}, u32[]{:S(2)}) copy-start(bf16[128,3,8,256]{3,2,1,0:T(8,128)(2,1)S(1)} %get-tuple-element.8) | copy-start | bytes 4718596
  11.0 11.5 %copy-start.2 = (f32[2,128,256]{2,1,0:T(8,128)S(1)}, f32[2,128,256]{2,1,0:T(8,128)}, u32[]{:S(2)}) copy-start(f32[2,128,256]{2,1,0:T(8,128)} %constant.6.clone.coarse_ref) | copy-start | bytes 786436
  11.0 11.5 %copy-start.4 = (f32[2,6,768]{2,1,0:T(8,128)S(1)}, f32[2,6,768]{2,1,0:T(8,128)}, u32[]{:S(2)}) copy-start(f32[2,6,768]{2,1,0:T(8,128)} %constant.7.clone.fine_ref) | copy-start | bytes 110596
  11.0 11.5 %copy-start.7 = (f32[8]{0:T(128)S(1)}, f32[8]{0:T(128)}, u32[]{:S(2)}) copy-start(f32[8]{0:T(128)} %gain_ref.3) | copy-start | bytes 100
  11.0 36.3 %all-to-all-start.1 = ((bf16[128,3,8,256]{3,2,1,0:T(8,128)(2,1)}), bf16[128,3,8,256]{3,2,1,0:T(8,128)(2,1)S(1)}, u32[]{:S(2)}, u32[]{:S(2)}) async-start(bf16[128,3,8,256]{3,2,1,0:T(8,128)(2,1)} %copy-done), calls=%async_computation.1 | async-start | bytes 3145728 | tf_op jit(solution)/shard_map/all_to_all | solution.py:182
  47.3 29.4 %all-to-all-start = ((bf16[128,3,8,256]{3,2,1,0:T(8,128)(2,1)}), bf16[128,3,8,256]{3,2,1,0:T(8,128)(2,1)S(1)}, u32[]{:S(2)}, u32[]{:S(2)}) async-start(bf16[128,3,8,256]{3,2,1,0:T(8,128)(2,1)} %odd.1), calls=%async_computation | async-start | bytes 3145728 | tf_op jit(solution)/shard_map/all_to_all | solution.py:192

commit v2 on v1

v2 whole, which is shorter than its diff:
```python
import math

import jax
import jax.numpy as jnp
import numpy as np
from jax import lax
from jax.experimental import pallas as pl
from jax.experimental.pallas import tpu as pltpu
from jax.sharding import PartitionSpec as P

INPUTS = 1024
FRAME = 1536
TAPS = 4
SPECTRA = 128
BLOCK = 128
CHANNELS = 768
DEVICES = 128
LOCAL = INPUTS // DEVICES
OWNED = CHANNELS // DEVICES
HALF = FRAME // 2
NBLK = INPUTS // BLOCK
PER = OWNED // 2
STEP = 16
SCALE = 1024.0
F32 = jnp.float32
BF16 = jnp.bfloat16
NT = (((1,), (1,)), ((), ()))


def pfb_window():
    total = TAPS * FRAME
    position = np.arange(total, dtype=np.float64)
    centred = (position - total / 2 + 0.5) / FRAME
    taper = 0.54 - 0.46 * np.cos(2.0 * math.pi * position / (total - 1))
    return (np.sinc(centred) * taper).reshape(TAPS, FRAME).astype(np.float32)


def twiddles():
    owner = np.outer(np.arange(DEVICES), np.arange(256)) % 256 * (2.0 * math.pi / 256)
    own = np.outer(np.arange(OWNED), np.arange(HALF)) % FRAME * (2.0 * math.pi / FRAME)
    norm = 1.0 / math.sqrt(FRAME)
    coarse = np.stack([np.cos(owner), -np.sin(owner)]) * norm
    fine = np.stack([np.cos(own), -np.sin(own)])
    return coarse.astype(np.float32), fine.astype(np.float32)


def make_table(parity, coarse_ref, fine_ref, table_ref):
    for block in range(HALF // 256):
        lanes = slice(block * 256, block * 256 + 256)
        for m in range(PER):
            j = 2 * m + parity
            fre = fine_ref[0, j : j + 1, lanes]
            fim = fine_ref[1, j : j + 1, lanes]
            base = (parity * PER + m) * 2 * DEVICES
            re = coarse_ref[0]
            im = coarse_ref[1]
            table_ref[base : base + DEVICES, lanes] = (re * fre - im * fim).astype(BF16)
            table_ref[base + DEVICES : base + 2 * DEVICES, lanes] = (re * fim + im * fre).astype(BF16)


def frames_of(b, frames_hbm, frames_ref, sem):
    if b == 0:
        rows = pl.ds(0, STEP + TAPS - 1)
    else:
        rows = pl.ds(b * STEP + TAPS - 1, STEP)
    return pltpu.make_async_copy(frames_hbm.at[rows], frames_ref.at[rows], sem.at[b])


def transform_kernel(
    frames_hbm, window_hbm, coarse_hbm, fine_hbm, gain_ref, out_hbm,
    frames_ref, window_ref, coarse_ref, fine_ref, folds_ref, folded_ref, table_ref, turned_ref, sent_ref, frame_sem, sem, out_sem,
):
    small = [
        pltpu.make_async_copy(window_hbm, window_ref, sem.at[0]),
        pltpu.make_async_copy(coarse_hbm, coarse_ref, sem.at[1]),
        pltpu.make_async_copy(fine_hbm, fine_ref, sem.at[2]),
    ]
    for copy in small:
        copy.start()
    loads = [frames_of(b, frames_hbm, frames_ref, frame_sem) for b in range(SPECTRA // STEP)]
    for load in loads:
        load.start()
    for copy in small[1:]:
        copy.wait()
    for parity in range(2):
        make_table(parity, coarse_ref, fine_ref, table_ref)
    small[0].wait()
    width = 128

    def body(b):
        s0 = b * STEP
        for block in range(HALF // width):
            acc = []
            for half in range(2):
                lanes = slice(half * HALF + block * width, half * HALF + block * width + width)
                frames = frames_ref[pl.ds(s0, STEP + TAPS - 1), :, lanes].astype(F32)
                total = window_ref[0, lanes][None, None, :] * frames[0:STEP]
                for tap in range(1, TAPS):
                    total = total + window_ref[tap, lanes][None, None, :] * frames[tap : tap + STEP]
                acc.append(total.reshape(STEP * LOCAL, width))
            here = pl.ds(s0 * LOCAL, STEP * LOCAL)
            folds_ref[0, block, here] = acc[0] + acc[1]
            folds_ref[1, block, here] = acc[0] - acc[1]

    for b in range(SPECTRA // STEP):
        loads[b].wait()
        body(b)
    for i in range(LOCAL):
        for parity in range(2):
            for block in range(HALF // width):
                lanes = slice(block * width, block * width + width)
                mine = slice(i * SPECTRA, (i + 1) * SPECTRA)
                folded_ref[parity, mine, lanes] = folds_ref[parity, block, pl.ds(i, SPECTRA, stride=LOCAL)].astype(BF16)
    stores = []
    for parity in range(2):
        top = parity * PER * 2 * DEVICES
        for pair in range(LOCAL // 2):
            rows = folded_ref[parity, pair * 256 : pair * 256 + 256, :]
            spec = lax.dot_general(table_ref[top : top + PER * 2 * DEVICES, :], rows, NT, preferred_element_type=F32)
            for m in range(PER):
                for ri in range(2):
                    base = (m * 2 + ri) * DEVICES
                    for side in range(2):
                        i = 2 * pair + side
                        gain = gain_ref[i] * SCALE
                        turned_ref[parity, m, ri, pl.ds(i, DEVICES, stride=LOCAL)] = (
                            spec[base : base + DEVICES, side * SPECTRA : (side + 1) * SPECTRA] * gain
                        )
        for m in range(PER):
            c = parity * PER + m
            for ri in range(2):
                sent_ref[:, c, :, ri * SPECTRA : (ri + 1) * SPECTRA] = (
                    turned_ref[parity, m, ri].reshape(DEVICES, LOCAL, SPECTRA).astype(BF16)
                )
            store = pltpu.make_async_copy(sent_ref.at[:, c], out_hbm.at[:, c], out_sem.at[c])
            store.start()
            stores.append(store)
    for store in stores:
        store.wait()


def prepare(c, slot, spectra_ref, volt_ref, turn_ref, scale_ref):
    volt = spectra_ref[:, c].reshape(INPUTS, 2 * SPECTRA)
    volt_ref[slot] = volt
    turn_ref[slot, :, :SPECTRA] = -volt[:, SPECTRA:]
    turn_ref[slot, :, SPECTRA:] = volt[:, :SPECTRA]
    wide = volt.astype(F32)
    power = jnp.sum(wide * wide, keepdims=True) * (1.0 / (SCALE * SCALE))
    scale = (1.0 / (power / (INPUTS * SPECTRA) + 1e-06)) * (1.0 / (SCALE * SCALE * SPECTRA))
    scale_ref[slot] = jnp.broadcast_to(scale, (8, 128))


def gram_kernel(spectra_ref, out_ref, volt_ref, turn_ref, scale_ref):
    c = pl.program_id(0)
    slot = c % 2

    @pl.when(c == 0)
    def _():
        prepare(0, 0, spectra_ref, volt_ref, turn_ref, scale_ref)

    scale = scale_ref[slot][:1]
    for cols in range(NBLK // 2):
        height = (2 * cols + 2) * BLOCK
        at = slice(cols * 256, cols * 256 + 256)
        for ri, right_ref in enumerate((volt_ref, turn_ref)):
            tiles = lax.dot_general(volt_ref[slot, :height], right_ref[slot, at], NT, preferred_element_type=F32)
            for r in range(2 * cols + 2):
                for side in range(2):
                    col = 2 * cols + side
                    if col < r:
                        continue
                    p = r * NBLK - r * (r - 1) // 2 + col - r
                    tile = tiles[r * BLOCK : (r + 1) * BLOCK, side * BLOCK : (side + 1) * BLOCK]
                    out_ref[p, ri] = (tile * scale).astype(BF16)
    prepare(jnp.minimum(c + 1, OWNED - 1), 1 - slot, spectra_ref, volt_ref, turn_ref, scale_ref)


def gram(received):
    npair = NBLK * (NBLK + 1) // 2
    return pl.pallas_call(
        gram_kernel,
        name="gram",
        grid=(OWNED,),
        in_specs=[pl.BlockSpec(memory_space=pltpu.VMEM)],
        out_specs=pl.BlockSpec((None, npair, 2, BLOCK, BLOCK), lambda c: (2 * (c % PER) + c // PER, 0, 0, 0, 0)),
        out_shape=jax.ShapeDtypeStruct((OWNED, npair, 2, BLOCK, BLOCK), BF16),
        scratch_shapes=[
            pltpu.VMEM((2, INPUTS, 2 * SPECTRA), BF16),
            pltpu.VMEM((2, INPUTS, 2 * SPECTRA), BF16),
            pltpu.VMEM((2, 8, 128), F32),
        ],
        compiler_params=pltpu.CompilerParams(vmem_limit_bytes=48 << 20),
    )(received)


def local(samples, input_gain):
    frames = samples.reshape(LOCAL, SPECTRA + TAPS - 1, FRAME).transpose(1, 0, 2)
    coarse, fine = (jnp.asarray(t) for t in twiddles())
    window = jnp.asarray(pfb_window())
    rows = LOCAL * SPECTRA
    hbm = pl.BlockSpec(memory_space=pltpu.HBM)
    outgoing = pl.pallas_call(
        transform_kernel,
        name="transform",
        in_specs=[hbm] * 4 + [pl.BlockSpec(memory_space=pltpu.SMEM)],
        out_specs=hbm,
        out_shape=jax.ShapeDtypeStruct((DEVICES, OWNED, LOCAL, 2 * SPECTRA), BF16),
        scratch_shapes=[
            pltpu.VMEM(frames.shape, BF16),
            pltpu.VMEM(window.shape, F32),
            pltpu.VMEM(coarse.shape, F32),
            pltpu.VMEM(fine.shape, F32),
            pltpu.VMEM((2, HALF // 128, rows, 128), F32),
            pltpu.VMEM((2, rows, HALF), BF16),
            pltpu.VMEM((2 * OWNED * DEVICES, HALF), BF16),
            pltpu.VMEM((2, PER, 2, DEVICES * LOCAL, SPECTRA), F32),
            pltpu.VMEM((DEVICES, OWNED, LOCAL, 2 * SPECTRA), BF16),
            pltpu.SemaphoreType.DMA((SPECTRA // STEP,)),
            pltpu.SemaphoreType.DMA((3,)),
            pltpu.SemaphoreType.DMA((OWNED,)),
        ],
        compiler_params=pltpu.CompilerParams(vmem_limit_bytes=56 << 20),
    )(frames, window, coarse, fine, input_gain)
    return gram(lax.all_to_all(outgoing, "dev", split_axis=0, concat_axis=0, tiled=True))


def solution(mesh):
    in_specs = (P("dev", None), P("dev"))
    out_specs = P("dev", None, None, None, None)
    return jax.shard_map(local, mesh=mesh, in_specs=in_specs, out_specs=out_specs, check_vma=False)
```

time: 82.3 us -> 71.8 us (0.87)
  blocking collectives: 0 us -> 53 us
  waiting for transfers between devices: 41.1 us -> 0 us
  starting transfers between devices: 15.9 us -> 0 us
  local copies, waits for them, and re-layouts: 4.29 us -> 0 us
  Pallas kernels: 20.6 us -> 18.6 us
    all_to_all x0 -> x1, blocking collectives: none -> 53 us  [local(): lax.all_to_all(outgoing, 'dev', split_axis=0, concat_axis=0, tiled=True)]
    all_to_all x2 -> x0, waiting for transfers between devices: 41.1 us -> none  [the longest x1 21.3 us: local(): even = move(even)]
    all_to_all x2 -> x0, starting transfers between devices: 15.9 us -> none  [the longest x1 11.5 us: local(): even = move(even)]
    unnamed x16 -> x0, local copies, waits for them, and re-layouts: 4.29 us -> none
    pallas_call x4 -> x2, Pallas kernels: 20.6 us -> 18.6 us  [the longest x1 10.1 us: local(): pl.pallas_call(transform_kernel, name='transform', in_specs=[hbm] * 4 + [...]
  transfers between devices with their start and end apart: 2 -> 0, of which waited for: 2 -> 0; matrix products, arithmetic and copies ran while one was open for 0% -> 0% of each run, Pallas kernels for 11% -> 0%
where the time goes in v2:
time: 71.8 us; the launch traced here: 71.6 us
  blocking collectives  53 us (74%)
  Pallas kernels  18.6 us (26%)
    all_to_all x1, blocking collectives, local(): lax.all_to_all(outgoing, 'dev', split_axis=0, concat_axis=0, tiled=True)  53 us
    pallas_call x1, Pallas kernels, local(): pl.pallas_call(transform_kernel, name='transform', in_specs=[hbm] * 4 + [...  10.1 us
    pallas_call x1, Pallas kernels, gram(): pl.pallas_call(gram_kernel, name='gram', grid=(OWNED,), in_specs=[pl.Bloc...  8.58 us

profile of v2, /device:TPU:1, one launch (start us, length us, event | category | flops | bytes accessed | tf_op | source)
XLA Modules:
  0.0 71.6 jit_solution(4362709485081575317)
XLA Ops:
  0.0 10.1 %transform.1 = bf16[128,6,8,256]{3,2,1,0:T(8,128)(2,1)} custom-call(bf16[131,8,1536]{2,1,0:T(8,128)(2,1)} %bitcast.3, f32[4,1536]{1,0:T(4,128)} %constant.8.clone.window_hbm, f32[2,128,256]{2,1,0:T(8,128)} %constant.6.clone.coarse_hbm, f32[2,6,768]{2,1,0:T(8,128)} %constant.7.clone.fine_hbm, f32[8]{0:T(128)} %gain_ref.1), custom_call_target="tpu_custom_call" | custom-call | tf_op jit(solution)/shard_map/transform/pallas_call | solution.py:202
  10.1 53.0 %all_to_all.5.spectra_ref = bf16[128,6,8,256]{3,2,1,0:T(8,128)(2,1)S(1)} all-to-all(bf16[128,6,8,256]{3,2,1,0:T(8,128)(2,1)} %transform.1), channel_id=1, replica_groups=mesh['dev'=128] {'dev'}, dimensions={0} | all-to-all | bytes 6291456 | tf_op jit(solution)/shard_map/all_to_all | solution.py:224
  63.0 8.6 %gram.1 = bf16[6,36,2,128,128]{4,3,2,1,0:T(8,128)(2,1)} custom-call(bf16[128,6,8,256]{3,2,1,0:T(8,128)(2,1)S(1)} %all_to_all.5.spectra_ref), custom_call_target="tpu_custom_call" | custom-call | tf_op jit(solution)/shard_map/gram/pallas_call | solution.py:180

commit v3 on v2

v3 whole, which is shorter than its diff:
```python
import math

import jax
import jax.numpy as jnp
import numpy as np
from jax import lax
from jax.experimental import pallas as pl
from jax.experimental.pallas import tpu as pltpu
from jax.sharding import PartitionSpec as P

INPUTS = 1024
FRAME = 1536
TAPS = 4
SPECTRA = 128
BLOCK = 128
CHANNELS = 768
DEVICES = 128
LOCAL = INPUTS // DEVICES
OWNED = CHANNELS // DEVICES
HALF = FRAME // 2
NBLK = INPUTS // BLOCK
PER = OWNED // 2
STEP = 16
PITCH = 9
SCALE = 1024.0
F32 = jnp.float32
BF16 = jnp.bfloat16
NT = (((1,), (1,)), ((), ()))


def pfb_window():
    total = TAPS * FRAME
    position = np.arange(total, dtype=np.float64)
    centred = (position - total / 2 + 0.5) / FRAME
    taper = 0.54 - 0.46 * np.cos(2.0 * math.pi * position / (total - 1))
    return (np.sinc(centred) * taper).reshape(TAPS, FRAME).astype(np.float32)


def dft_table():
    parity, m, owner = np.meshgrid(np.arange(2), np.arange(PER), np.arange(DEVICES), indexing="ij")
    channel = OWNED * owner + 2 * m + parity
    phase = channel[..., None] * np.arange(HALF) % FRAME
    angle = 2.0 * math.pi / FRAME * phase.astype(np.float64)
    table = np.stack([np.cos(angle), -np.sin(angle)], axis=2) / math.sqrt(FRAME)
    return table.reshape(2 * CHANNELS, HALF).astype(np.float32).astype(jnp.bfloat16)


def frames_of(b, frames_hbm, frames_ref, sem):
    if b == 0:
        rows = pl.ds(0, STEP + TAPS - 1)
    else:
        rows = pl.ds(b * STEP + TAPS - 1, STEP)
    return pltpu.make_async_copy(frames_hbm.at[rows], frames_ref.at[rows], sem.at[b])


def filter_pair(pair, raw_ref, window_ref, gain_ref, folded_ref):
    for side in range(2):
        i = 2 * pair + side
        gain = gain_ref[i] * SCALE
        for block in range(HALF // 128):
            acc = []
            for half in range(2):
                tile = half * (HALF // 128) + block
                lanes = slice(tile * 128, tile * 128 + 128)
                total = None
                for tap in range(TAPS):
                    weight = window_ref[tap : tap + 1, lanes] * gain
                    term = weight * raw_ref[tile, pl.ds(tap * PITCH + i, SPECTRA, stride=PITCH)]
                    total = term if total is None else total + term
                acc.append(total)
            lanes = slice(block * 128, block * 128 + 128)
            mine = slice(i * SPECTRA, (i + 1) * SPECTRA)
            folded_ref[0, mine, lanes] = (acc[0] + acc[1]).astype(BF16)
            folded_ref[1, mine, lanes] = (acc[0] - acc[1]).astype(BF16)


def transform_pair(pair, parity, table_ref, folded_ref, turned_ref):
    rows = folded_ref[parity, pair * 256 : pair * 256 + 256, :]
    top = parity * CHANNELS
    spec = lax.dot_general(table_ref[top : top + CHANNELS, :], rows, NT, preferred_element_type=F32)
    for m in range(PER):
        for ri in range(2):
            base = (m * 2 + ri) * DEVICES
            for side in range(2):
                turned_ref[parity * PER + m, ri, pl.ds(2 * pair + side, DEVICES, stride=PITCH)] = (
                    spec[base : base + DEVICES, side * SPECTRA : (side + 1) * SPECTRA]
                )


def pack(parity, turned_ref, sent_ref):
    for c in range(parity * PER, (parity + 1) * PER):
        for owner in range(DEVICES):
            for ri in range(2):
                rows = turned_ref[c, ri, owner * PITCH : owner * PITCH + LOCAL]
                sent_ref[owner, c, :, ri * SPECTRA : (ri + 1) * SPECTRA] = rows.astype(BF16)


def transform_kernel(
    frames_hbm, window_hbm, table_hbm, gain_ref, out_hbm,
    frames_ref, window_ref, table_ref, raw_ref, folded_ref, turned_ref, sent_ref, frame_sem, sem, out_sem,
):
    window_load = pltpu.make_async_copy(window_hbm, window_ref, sem.at[0])
    window_load.start()
    loads = [frames_of(b, frames_hbm, frames_ref, frame_sem) for b in range(SPECTRA // STEP)]
    for load in loads:
        load.start()
    table_load = pltpu.make_async_copy(table_hbm, table_ref, sem.at[1])
    table_load.start()
    for b, load in enumerate(loads):
        load.wait()
        first = b * STEP + TAPS - 1 if b else 0
        for f in range(first, (b + 1) * STEP + TAPS - 1):
            for tile in range(FRAME // 128):
                raw_ref[tile, f * PITCH : f * PITCH + LOCAL] = frames_ref[f, :, tile * 128 : tile * 128 + 128].astype(F32)
    window_load.wait()
    filter_pair(0, raw_ref, window_ref, gain_ref, folded_ref)
    table_load.wait()
    stores = []
    for pair in range(LOCAL // 2):
        transform_pair(pair, 0, table_ref, folded_ref, turned_ref)
        if pair + 1 < LOCAL // 2:
            filter_pair(pair + 1, raw_ref, window_ref, gain_ref, folded_ref)
        else:
            pack(0, turned_ref, sent_ref)
        transform_pair(pair, 1, table_ref, folded_ref, turned_ref)
    for parity in range(2):
        if parity:
            pack(parity, turned_ref, sent_ref)
        chans = pl.ds(parity * PER, PER)
        store = pltpu.make_async_copy(sent_ref.at[:, chans], out_hbm.at[:, chans], out_sem.at[parity])
        store.start()
        stores.append(store)
    for store in stores:
        store.wait()


def prepare(c, slot, spectra_ref, volt_ref, turn_ref, scale_ref):
    volt = spectra_ref[:, c].reshape(INPUTS, 2 * SPECTRA)
    volt_ref[slot] = volt
    turn_ref[slot, :, :SPECTRA] = -volt[:, SPECTRA:]
    turn_ref[slot, :, SPECTRA:] = volt[:, :SPECTRA]
    wide = volt.astype(F32)
    power = jnp.sum(wide * wide, keepdims=True) * (1.0 / (SCALE * SCALE))
    scale = (1.0 / (power / (INPUTS * SPECTRA) + 1e-06)) * (1.0 / (SCALE * SCALE * SPECTRA))
    scale_ref[slot] = jnp.broadcast_to(scale, (8, 128))


def gram_kernel(spectra_ref, out_ref, volt_ref, turn_ref, scale_ref):
    c = pl.program_id(0)
    slot = c % 2

    @pl.when(c == 0)
    def _():
        prepare(0, 0, spectra_ref, volt_ref, turn_ref, scale_ref)

    scale = scale_ref[slot][:1]
    for cols in range(NBLK // 2):
        height = (2 * cols + 2) * BLOCK
        at = slice(cols * 256, cols * 256 + 256)
        for ri, right_ref in enumerate((volt_ref, turn_ref)):
            tiles = lax.dot_general(volt_ref[slot, :height], right_ref[slot, at], NT, preferred_element_type=F32)
            for r in range(2 * cols + 2):
                for side in range(2):
                    col = 2 * cols + side
                    if col < r:
                        continue
                    p = r * NBLK - r * (r - 1) // 2 + col - r
                    tile = tiles[r * BLOCK : (r + 1) * BLOCK, side * BLOCK : (side + 1) * BLOCK]
                    out_ref[p, ri] = (tile * scale).astype(BF16)
    prepare(jnp.minimum(c + 1, OWNED - 1), 1 - slot, spectra_ref, volt_ref, turn_ref, scale_ref)


def gram(received):
    npair = NBLK * (NBLK + 1) // 2
    return pl.pallas_call(
        gram_kernel,
        name="gram",
        grid=(OWNED,),
        in_specs=[pl.BlockSpec(memory_space=pltpu.VMEM)],
        out_specs=pl.BlockSpec((None, npair, 2, BLOCK, BLOCK), lambda c: (2 * (c % PER) + c // PER, 0, 0, 0, 0)),
        out_shape=jax.ShapeDtypeStruct((OWNED, npair, 2, BLOCK, BLOCK), BF16),
        scratch_shapes=[
            pltpu.VMEM((2, INPUTS, 2 * SPECTRA), BF16),
            pltpu.VMEM((2, INPUTS, 2 * SPECTRA), BF16),
            pltpu.VMEM((2, 8, 128), F32),
        ],
        compiler_params=pltpu.CompilerParams(vmem_limit_bytes=48 << 20),
    )(received)


def local(samples, input_gain):
    frames = samples.reshape(LOCAL, SPECTRA + TAPS - 1, FRAME).transpose(1, 0, 2)
    table = jnp.asarray(dft_table())
    window = jnp.asarray(pfb_window())
    rows = LOCAL * SPECTRA
    hbm = pl.BlockSpec(memory_space=pltpu.HBM)
    outgoing = pl.pallas_call(
        transform_kernel,
        name="transform",
        in_specs=[hbm] * 3 + [pl.BlockSpec(memory_space=pltpu.SMEM)],
        out_specs=hbm,
        out_shape=jax.ShapeDtypeStruct((DEVICES, OWNED, LOCAL, 2 * SPECTRA), BF16),
        scratch_shapes=[
            pltpu.VMEM(frames.shape, BF16),
            pltpu.VMEM(window.shape, F32),
            pltpu.VMEM(table.shape, BF16),
            pltpu.VMEM((FRAME // 128, pl.cdiv(frames.shape[0] * PITCH, 8) * 8, 128), F32),
            pltpu.VMEM((2, rows, HALF), BF16),
            pltpu.VMEM((OWNED, 2, DEVICES * PITCH, SPECTRA), F32),
            pltpu.VMEM((DEVICES, OWNED, LOCAL, 2 * SPECTRA), BF16),
            pltpu.SemaphoreType.DMA((SPECTRA // STEP,)),
            pltpu.SemaphoreType.DMA((2,)),
            pltpu.SemaphoreType.DMA((2,)),
        ],
        compiler_params=pltpu.CompilerParams(vmem_limit_bytes=56 << 20),
    )(frames, window, table, input_gain)
    return gram(lax.all_to_all(outgoing, "dev", split_axis=0, concat_axis=0, tiled=True))


def solution(mesh):
    in_specs = (P("dev", None), P("dev"))
    out_specs = P("dev", None, None, None, None)
    return jax.shard_map(local, mesh=mesh, in_specs=in_specs, out_specs=out_specs, check_vma=False)
```

time: 71.8 us -> 70.1 us (0.976)
  Pallas kernels: 18.6 us -> 16.9 us
    pallas_call x1, Pallas kernels: 10.1 us -> 8.34 us  [local(): pl.pallas_call(transform_kernel, name='transform', in_specs=[hbm] * 3 + [...]
where the time goes in v3:
time: 70.1 us; the launch traced here: 69.9 us
  blocking collectives  53 us (76%)
  Pallas kernels  16.9 us (24%)
    all_to_all x1, blocking collectives, local(): lax.all_to_all(outgoing, 'dev', split_axis=0, concat_axis=0, tiled=True)  53 us
    pallas_call x1, Pallas kernels, gram(): pl.pallas_call(gram_kernel, name='gram', grid=(OWNED,), in_specs=[pl.Bloc...  8.58 us
    pallas_call x1, Pallas kernels, local(): pl.pallas_call(transform_kernel, name='transform', in_specs=[hbm] * 3 + [...  8.34 us

profile of v3, /device:TPU:1, one launch (start us, length us, event | category | flops | bytes accessed | tf_op | source)
XLA Modules:
  0.0 69.9 jit_solution(13040552045155247920)
XLA Ops:
  0.0 8.3 %transform.1 = bf16[128,6,8,256]{3,2,1,0:T(8,128)(2,1)} custom-call(bf16[131,8,1536]{2,1,0:T(8,128)(2,1)} %bitcast.3, f32[4,1536]{1,0:T(4,128)} %constant.5.clone.window_hbm, bf16[1536,768]{1,0:T(8,128)(2,1)} %constant.4.clone.table_hbm, f32[8]{0:T(128)} %gain_ref.1), custom_call_target="tpu_custom_call" | custom-call | tf_op jit(solution)/shard_map/transform/pallas_call | solution.py:197
  8.4 53.0 %all_to_all.5.spectra_ref = bf16[128,6,8,256]{3,2,1,0:T(8,128)(2,1)S(1)} all-to-all(bf16[128,6,8,256]{3,2,1,0:T(8,128)(2,1)} %transform.1), channel_id=1, replica_groups=mesh['dev'=128] {'dev'}, dimensions={0} | all-to-all | bytes 6291456 | tf_op jit(solution)/shard_map/all_to_all | solution.py:217
  61.3 8.6 %gram.1 = bf16[6,36,2,128,128]{4,3,2,1,0:T(8,128)(2,1)} custom-call(bf16[128,6,8,256]{3,2,1,0:T(8,128)(2,1)S(1)} %all_to_all.5.spectra_ref), custom_call_target="tpu_custom_call" | custom-call | tf_op jit(solution)/shard_map/gram/pallas_call | solution.py:175

commit v4 on v3

--- a/solution.py
+++ b/solution.py
@@ -74,7 +74,7 @@
             folded_ref[1, mine, lanes] = (acc[0] - acc[1]).astype(BF16)
 
 
-def transform_pair(pair, parity, table_ref, folded_ref, turned_ref):
+def transform_pair(pair, parity, table_ref, folded_ref, turned_refs):
     rows = folded_ref[parity, pair * 256 : pair * 256 + 256, :]
     top = parity * CHANNELS
     spec = lax.dot_general(table_ref[top : top + CHANNELS, :], rows, NT, preferred_element_type=F32)
@@ -82,23 +82,30 @@
         for ri in range(2):
             base = (m * 2 + ri) * DEVICES
             for side in range(2):
-                turned_ref[parity * PER + m, ri, pl.ds(2 * pair + side, DEVICES, stride=PITCH)] = (
+                turned_refs[parity][m, ri, pl.ds(2 * pair + side, DEVICES, stride=PITCH)] = (
                     spec[base : base + DEVICES, side * SPECTRA : (side + 1) * SPECTRA]
                 )
 
 
-def pack(parity, turned_ref, sent_ref):
-    for c in range(parity * PER, (parity + 1) * PER):
-        for owner in range(DEVICES):
-            for ri in range(2):
-                rows = turned_ref[c, ri, owner * PITCH : owner * PITCH + LOCAL]
-                sent_ref[owner, c, :, ri * SPECTRA : (ri + 1) * SPECTRA] = rows.astype(BF16)
+def pack(c, turned_refs, sent_refs, out_hbm, out_sem):
+    turned_ref = turned_refs[c // PER]
+    sent_ref = sent_refs[c // PER]
+    m = c % PER
+    for owner in range(DEVICES):
+        for ri in range(2):
+            rows = turned_ref[m, ri, owner * PITCH : owner * PITCH + LOCAL]
+            sent_ref[owner, m, :, ri * SPECTRA : (ri + 1) * SPECTRA] = rows.astype(BF16)
+    store = pltpu.make_async_copy(sent_ref.at[:, m], out_hbm.at[:, c], out_sem.at[c])
+    store.start()
+    return store
 
 
 def transform_kernel(
     frames_hbm, window_hbm, table_hbm, gain_ref, out_hbm,
-    frames_ref, window_ref, table_ref, raw_ref, folded_ref, turned_ref, sent_ref, frame_sem, sem, out_sem,
+    frames_ref, window_ref, table_ref, raw_ref, folded_ref, turned_even, turned_odd, sent_even, sent_odd, frame_sem, sem, out_sem,
 ):
+    turned_refs = (turned_even, turned_odd)
+    sent_refs = (sent_even, sent_odd)
     window_load = pltpu.make_async_copy(window_hbm, window_ref, sem.at[0])
     window_load.start()
     loads = [frames_of(b, frames_hbm, frames_ref, frame_sem) for b in range(SPECTRA // STEP)]
@@ -117,72 +124,83 @@
     table_load.wait()
     stores = []
     for pair in range(LOCAL // 2):
-        transform_pair(pair, 0, table_ref, folded_ref, turned_ref)
+        transform_pair(pair, 0, table_ref, folded_ref, turned_refs)
         if pair + 1 < LOCAL // 2:
             filter_pair(pair + 1, raw_ref, window_ref, gain_ref, folded_ref)
         else:
-            pack(0, turned_ref, sent_ref)
-        transform_pair(pair, 1, table_ref, folded_ref, turned_ref)
-    for parity in range(2):
-        if parity:
-            pack(parity, turned_ref, sent_ref)
-        chans = pl.ds(parity * PER, PER)
-        store = pltpu.make_async_copy(sent_ref.at[:, chans], out_hbm.at[:, chans], out_sem.at[parity])
-        store.start()
-        stores.append(store)
+            for c in range(PER):
+                stores.append(pack(c, turned_refs, sent_refs, out_hbm, out_sem))
+        transform_pair(pair, 1, table_ref, folded_ref, turned_refs)
+    for c in range(PER, OWNED):
+        stores.append(pack(c, turned_refs, sent_refs, out_hbm, out_sem))
     for store in stores:
         store.wait()
 
 
-def prepare(c, slot, spectra_ref, volt_ref, turn_ref, scale_ref):
+def prepare(c, spectra_ref, volt_ref, turn_ref):
+    slot = c % 2
     volt = spectra_ref[:, c].reshape(INPUTS, 2 * SPECTRA)
     volt_ref[slot] = volt
     turn_ref[slot, :, :SPECTRA] = -volt[:, SPECTRA:]
     turn_ref[slot, :, SPECTRA:] = volt[:, :SPECTRA]
     wide = volt.astype(F32)
-    power = jnp.sum(wide * wide, keepdims=True) * (1.0 / (SCALE * SCALE))
-    scale = (1.0 / (power / (INPUTS * SPECTRA) + 1e-06)) * (1.0 / (SCALE * SCALE * SPECTRA))
-    scale_ref[slot] = jnp.broadcast_to(scale, (8, 128))
-
-
-def gram_kernel(spectra_ref, out_ref, volt_ref, turn_ref, scale_ref):
-    c = pl.program_id(0)
-    slot = c % 2
-
-    @pl.when(c == 0)
-    def _():
-        prepare(0, 0, spectra_ref, volt_ref, turn_ref, scale_ref)
-
-    scale = scale_ref[slot][:1]
-    for cols in range(NBLK // 2):
-        height = (2 * cols + 2) * BLOCK
-        at = slice(cols * 256, cols * 256 + 256)
-        for ri, right_ref in enumerate((volt_ref, turn_ref)):
-            tiles = lax.dot_general(volt_ref[slot, :height], right_ref[slot, at], NT, preferred_element_type=F32)
-            for r in range(2 * cols + 2):
-                for side in range(2):
-                    col = 2 * cols + side
-                    if col < r:
-                        continue
-                    p = r * NBLK - r * (r - 1) // 2 + col - r
-                    tile = tiles[r * BLOCK : (r + 1) * BLOCK, side * BLOCK : (side + 1) * BLOCK]
-                    out_ref[p, ri] = (tile * scale).astype(BF16)
-    prepare(jnp.minimum(c + 1, OWNED - 1), 1 - slot, spectra_ref, volt_ref, turn_ref, scale_ref)
+    part = jnp.sum((wide * wide).reshape(8, INPUTS // 64, 8, 2 * SPECTRA), axis=1)
+    power = jnp.sum(jnp.sum(part, axis=0), keepdims=True) * (1.0 / (SCALE * SCALE))
+    return (1.0 / (power / (INPUTS * SPECTRA) + 1e-06)) * (1.0 / (SCALE * SCALE * SPECTRA))
+
+
+def pair_of(row, col):
+    return row * NBLK - row * (row - 1) // 2 + col - row
+
+
+def gram_kernel(spectra_ref, out_hbm, volt_ref, turn_ref, tiles_ref, sem, last_sem):
+    scale = prepare(0, spectra_ref, volt_ref, turn_ref)
+    stores = []
+    for c in range(OWNED):
+        slot = c % 2
+        channel = 2 * (c % PER) + c // PER
+        following = None
+        for cols in reversed(range(NBLK // 2)):
+            height = (2 * cols + 2) * BLOCK
+            at = slice(cols * 256, cols * 256 + 256)
+            for ri, right_ref in enumerate((volt_ref, turn_ref)):
+                tiles = lax.dot_general(volt_ref[slot, :height], right_ref[slot, at], NT, preferred_element_type=F32)
+                for row in range(2 * cols + 2):
+                    for side in range(2):
+                        col = 2 * cols + side
+                        if col >= row:
+                            tile = tiles[row * BLOCK : (row + 1) * BLOCK, side * BLOCK : (side + 1) * BLOCK]
+                            tiles_ref[c, pair_of(row, col), ri] = (tile * scale).astype(BF16)
+            if following is None and c + 1 < OWNED:
+                following = prepare(c + 1, spectra_ref, volt_ref, turn_ref)
+            if c + 1 == OWNED:
+                for row in range(2 * cols + 2):
+                    first = max(row, 2 * cols)
+                    pairs = pl.ds(pair_of(row, first), 2 * cols + 2 - first)
+                    stores.append(pltpu.make_async_copy(tiles_ref.at[c, pairs], out_hbm.at[channel, pairs], last_sem.at[pair_of(row, first)]))
+                    stores[-1].start()
+        if c + 1 < OWNED:
+            stores.append(pltpu.make_async_copy(tiles_ref.at[c], out_hbm.at[channel], sem.at[c]))
+            stores[-1].start()
+        scale = following
+    for store in stores:
+        store.wait()
 
 
 def gram(received):
-    npair = NBLK * (NBLK + 1) // 2
+    shape = (OWNED, NBLK * (NBLK + 1) // 2, 2, BLOCK, BLOCK)
     return pl.pallas_call(
         gram_kernel,
         name="gram",
-        grid=(OWNED,),
         in_specs=[pl.BlockSpec(memory_space=pltpu.VMEM)],
-        out_specs=pl.BlockSpec((None, npair, 2, BLOCK, BLOCK), lambda c: (2 * (c % PER) + c // PER, 0, 0, 0, 0)),
-        out_shape=jax.ShapeDtypeStruct((OWNED, npair, 2, BLOCK, BLOCK), BF16),
+        out_specs=pl.BlockSpec(memory_space=pltpu.HBM),
+        out_shape=jax.ShapeDtypeStruct(shape, BF16),
         scratch_shapes=[
             pltpu.VMEM((2, INPUTS, 2 * SPECTRA), BF16),
             pltpu.VMEM((2, INPUTS, 2 * SPECTRA), BF16),
-            pltpu.VMEM((2, 8, 128), F32),
+            pltpu.VMEM(shape, BF16),
+            pltpu.SemaphoreType.DMA((OWNED,)),
+            pltpu.SemaphoreType.DMA(shape[1:2]),
         ],
         compiler_params=pltpu.CompilerParams(vmem_limit_bytes=48 << 20),
     )(received)
@@ -206,11 +224,11 @@
             pltpu.VMEM(table.shape, BF16),
             pltpu.VMEM((FRAME // 128, pl.cdiv(frames.shape[0] * PITCH, 8) * 8, 128), F32),
             pltpu.VMEM((2, rows, HALF), BF16),
-            pltpu.VMEM((OWNED, 2, DEVICES * PITCH, SPECTRA), F32),
-            pltpu.VMEM((DEVICES, OWNED, LOCAL, 2 * SPECTRA), BF16),
+            *[pltpu.VMEM((PER, 2, DEVICES * PITCH, SPECTRA), F32)] * 2,
+            *[pltpu.VMEM((DEVICES, PER, LOCAL, 2 * SPECTRA), BF16)] * 2,
             pltpu.SemaphoreType.DMA((SPECTRA // STEP,)),
             pltpu.SemaphoreType.DMA((2,)),
-            pltpu.SemaphoreType.DMA((2,)),
+            pltpu.SemaphoreType.DMA((OWNED,)),
         ],
         compiler_params=pltpu.CompilerParams(vmem_limit_bytes=56 << 20),
     )(frames, window, table, input_gain)

time: 70.1 us -> 67.7 us (0.966)
  Pallas kernels: 16.9 us -> 14.5 us
    pallas_call x1, Pallas kernels: 8.58 us -> 6.46 us  [gram(): pl.pallas_call(gram_kernel, name='gram', in_specs=[pl.BlockSpec(memory_sp...]
where the time goes in v4:
time: 67.7 us; the launch traced here: 67.5 us
  blocking collectives  53 us (78%)
  Pallas kernels  14.5 us (21%)
    all_to_all x1, blocking collectives, local(): lax.all_to_all(outgoing, 'dev', split_axis=0, concat_axis=0, tiled=True)  53 us
    pallas_call x1, Pallas kernels, local(): pl.pallas_call(transform_kernel, name='transform', in_specs=[hbm] * 3 + [...  8.08 us
    pallas_call x1, Pallas kernels, gram(): pl.pallas_call(gram_kernel, name='gram', in_specs=[pl.BlockSpec(memory_sp...  6.46 us

profile of v4, /device:TPU:1, one launch (start us, length us, event | category | flops | bytes accessed | tf_op | source)
XLA Modules:
  0.0 67.5 jit_solution(15691811766749197168)
XLA Ops:
  0.0 8.1 %transform.1 = bf16[128,6,8,256]{3,2,1,0:T(8,128)(2,1)} custom-call(bf16[131,8,1536]{2,1,0:T(8,128)(2,1)} %bitcast.3, f32[4,1536]{1,0:T(4,128)} %constant.5.clone.window_hbm, bf16[1536,768]{1,0:T(8,128)(2,1)} %constant.4.clone.table_hbm, f32[8]{0:T(128)} %gain_ref.1), custom_call_target="tpu_custom_call" | custom-call | tf_op jit(solution)/shard_map/transform/pallas_call | solution.py:215
  8.1 53.0 %all_to_all.5.spectra_ref = bf16[128,6,8,256]{3,2,1,0:T(8,128)(2,1)S(1)} all-to-all(bf16[128,6,8,256]{3,2,1,0:T(8,128)(2,1)} %transform.1), channel_id=1, replica_groups=mesh['dev'=128] {'dev'}, dimensions={0} | all-to-all | bytes 6291456 | tf_op jit(solution)/shard_map/all_to_all | solution.py:235
  61.1 6.5 %gram.1 = bf16[6,36,2,128,128]{4,3,2,1,0:T(8,128)(2,1)} custom-call(bf16[128,6,8,256]{3,2,1,0:T(8,128)(2,1)S(1)} %all_to_all.5.spectra_ref), custom_call_target="tpu_custom_call" | custom-call | tf_op jit(solution)/shard_map/gram/pallas_call | solution.py:192

commit v5 on v4

--- a/solution.py
+++ b/solution.py
@@ -101,13 +101,15 @@
 
 
 def transform_kernel(
-    frames_hbm, window_hbm, table_hbm, gain_ref, out_hbm,
-    frames_ref, window_ref, table_ref, raw_ref, folded_ref, turned_even, turned_odd, sent_even, sent_odd, frame_sem, sem, out_sem,
+    frames_hbm, window_hbm, table_hbm, gain_hbm, out_hbm,
+    gain_ref, frames_ref, window_ref, table_ref, raw_ref, folded_ref, turned_even, turned_odd, sent_even, sent_odd, frame_sem, sem, out_sem,
 ):
     turned_refs = (turned_even, turned_odd)
     sent_refs = (sent_even, sent_odd)
     window_load = pltpu.make_async_copy(window_hbm, window_ref, sem.at[0])
     window_load.start()
+    gain_load = pltpu.make_async_copy(gain_hbm, gain_ref, sem.at[2])
+    gain_load.start()
     loads = [frames_of(b, frames_hbm, frames_ref, frame_sem) for b in range(SPECTRA // STEP)]
     for load in loads:
         load.start()
@@ -120,6 +122,7 @@
             for tile in range(FRAME // 128):
                 raw_ref[tile, f * PITCH : f * PITCH + LOCAL] = frames_ref[f, :, tile * 128 : tile * 128 + 128].astype(F32)
     window_load.wait()
+    gain_load.wait()
     filter_pair(0, raw_ref, window_ref, gain_ref, folded_ref)
     table_load.wait()
     stores = []
@@ -215,10 +218,11 @@
     outgoing = pl.pallas_call(
         transform_kernel,
         name="transform",
-        in_specs=[hbm] * 3 + [pl.BlockSpec(memory_space=pltpu.SMEM)],
+        in_specs=[hbm] * 4,
         out_specs=hbm,
         out_shape=jax.ShapeDtypeStruct((DEVICES, OWNED, LOCAL, 2 * SPECTRA), BF16),
         scratch_shapes=[
+            pltpu.SMEM((LOCAL,), F32),
             pltpu.VMEM(frames.shape, BF16),
             pltpu.VMEM(window.shape, F32),
             pltpu.VMEM(table.shape, BF16),
@@ -227,7 +231,7 @@
             *[pltpu.VMEM((PER, 2, DEVICES * PITCH, SPECTRA), F32)] * 2,
             *[pltpu.VMEM((DEVICES, PER, LOCAL, 2 * SPECTRA), BF16)] * 2,
             pltpu.SemaphoreType.DMA((SPECTRA // STEP,)),
-            pltpu.SemaphoreType.DMA((2,)),
+            pltpu.SemaphoreType.DMA((3,)),
             pltpu.SemaphoreType.DMA((OWNED,)),
         ],
         compiler_params=pltpu.CompilerParams(vmem_limit_bytes=56 << 20),

time: 67.7 us -> 67.1 us (level)
  no operation moved by 1% of the time
where the time goes in v5:
time: 67.1 us; the launch traced here: 66.9 us
  blocking collectives  53 us (79%)
  Pallas kernels  13.9 us (21%)
    all_to_all x1, blocking collectives, local(): lax.all_to_all(outgoing, 'dev', split_axis=0, concat_axis=0, tiled=True)  53 us
    pallas_call x1, Pallas kernels, local(): pl.pallas_call(transform_kernel, name='transform', in_specs=[hbm] * 4, ou...  7.43 us
    pallas_call x1, Pallas kernels, gram(): pl.pallas_call(gram_kernel, name='gram', in_specs=[pl.BlockSpec(memory_sp...  6.46 us

profile of v5, /device:TPU:1, one launch (start us, length us, event | category | flops | bytes accessed | tf_op | source)
XLA Modules:
  0.0 66.9 jit_solution(4915544374738301249)
XLA Ops:
  0.0 7.4 %transform.1 = bf16[128,6,8,256]{3,2,1,0:T(8,128)(2,1)} custom-call(bf16[131,8,1536]{2,1,0:T(8,128)(2,1)} %bitcast.3, f32[4,1536]{1,0:T(4,128)} %constant.5.clone.window_hbm, bf16[1536,768]{1,0:T(8,128)(2,1)} %constant.4.clone.table_hbm, f32[8]{0:T(128)} %gain_hbm.1), custom_call_target="tpu_custom_call" | custom-call | tf_op jit(solution)/shard_map/transform/pallas_call | solution.py:218
  7.4 53.0 %all_to_all.5.spectra_ref = bf16[128,6,8,256]{3,2,1,0:T(8,128)(2,1)S(1)} all-to-all(bf16[128,6,8,256]{3,2,1,0:T(8,128)(2,1)} %transform.1), channel_id=1, replica_groups=mesh['dev'=128] {'dev'}, dimensions={0} | all-to-all | bytes 6291456 | tf_op jit(solution)/shard_map/all_to_all | solution.py:239
  60.4 6.5 %gram.1 = bf16[6,36,2,128,128]{4,3,2,1,0:T(8,128)(2,1)} custom-call(bf16[128,6,8,256]{3,2,1,0:T(8,128)(2,1)S(1)} %all_to_all.5.spectra_ref), custom_call_target="tpu_custom_call" | custom-call | tf_op jit(solution)/shard_map/gram/pallas_call | solution.py:195
